TPU v7x, 256 devices: a whole 4x4x8 slice. The times are simulated.
256 devices in a mesh: subj: 8 (over y_hi, x), cortex: 32 (over y_lo, z, core).
Axes of the slice: x: 4, y: 4 (y_hi: 2, y_lo: 2; y = y_hi * 2 + y_lo), z: 8, core: 2. Of those that a mesh axis runs over, the one named last changes fastest.
Arguments:
- series: bfloat16 [16, 1024, 8192], P('subj', None, 'cortex'), may hold values from -6 to 6
- template: bfloat16 [1024, 8192], P(None, 'cortex'), may hold values from -6 to 6
- sl_blocks: int32 [64, 3], P('cortex'), may hold values from 0 to 63, as said below
Outputs:
- template_new: float32 [1024, 8192], P(None, 'cortex')
Inputs may be any that keep to these rules, and one draw needn't show every extreme that they name: sl_blocks[g, 0] = g; the other two entries of row g are distinct, differ from g, and lie between (g // 2 - 1) * 2 and (g // 2 + 2) * 2 - 1.
All inputs are finite; a program needn't handle non-finite values.
Results may differ from a plain program's by a relative error of at most 0.0024.
Values may be sent and summed in bfloat16 or wider, within the bound.
A program may use at most 64 MiB of HBM per device.

v0:
```python
import jax
import jax.numpy as jnp
from jax import lax
from jax.sharding import PartitionSpec as P

BLOCK = 128
NS_STEPS = 8
BLK_DEV = 2
RIDGE_SHIFT = 0.1
NORM_EPSILON = 1e-06


def with_halo(cells, sides, width):
    for axis, dim in sides:
        count = lax.axis_size(axis)
        ends = count - 1
        head = lax.slice_in_dim(cells, 0, width, axis=dim)
        tail = lax.slice_in_dim(cells, cells.shape[dim] - width, cells.shape[dim], axis=dim)
        cells = jnp.concatenate(
            [
                lax.ppermute(tail, axis, [(i, (i + 1) % count) for i in range(ends)]),
                cells,
                lax.ppermute(head, axis, [((i + 1) % count, i) for i in range(ends)]),
            ],
            axis=dim,
        )
    return cells


def in_order(tiles, dim):
    shape = list(tiles.shape[1:])
    shape[dim] *= tiles.shape[0]
    return jnp.moveaxis(tiles, 0, dim).reshape(shape)


def copy_for_each(x, axis):
    length = lax.axis_size(axis)
    return lax.all_to_all(jnp.broadcast_to(x[None], (length, *x.shape)), axis, 0, 0, tiled=True)


def gathered_copies(x, axis, dim):
    return in_order(copy_for_each(x, axis), dim)


def from_behind(block, axis, distance):
    devices = range(lax.axis_size(axis))
    route = [(i - distance, i) for i in devices if i - distance in devices]
    return lax.ppermute(block, axis, route)


def body(series, template, sl_blocks):
    subj_count = series.shape[0]
    frame_count = series.shape[1]
    width_dev = series.shape[2]
    halo_data = with_halo(series, (("cortex", 2),), width_dev)
    halo_tmpl = with_halo(template, (("cortex", 1),), width_dev)
    all_lists = gathered_copies(sl_blocks, "cortex", 0)
    position = lax.axis_index("cortex")
    window_blocks = 3 * BLK_DEV
    window_ids = (sl_blocks - (position - 1) * BLK_DEV).reshape(-1)
    data_blocks = halo_data.reshape(subj_count, frame_count, window_blocks, BLOCK)
    tmpl_blocks = halo_tmpl.reshape(frame_count, window_blocks, BLOCK)
    subj_tiles = jnp.take(data_blocks, window_ids, axis=2).reshape(
        subj_count, frame_count, BLK_DEV, 3 * BLOCK
    )
    tmpl_tiles = jnp.take(tmpl_blocks, window_ids, axis=1).reshape(frame_count, BLK_DEV, 3 * BLOCK)
    identity = jnp.eye(3 * BLOCK, dtype=jnp.float32)
    cross_prod = jnp.einsum(
        "sfka,fkb->skab", subj_tiles, tmpl_tiles, preferred_element_type=jnp.float32
    )
    cross_prod = cross_prod / frame_count + RIDGE_SHIFT * identity
    squares = jnp.sum(cross_prod * cross_prod, axis=(2, 3), keepdims=True)
    polar_map = (cross_prod / jnp.sqrt(squares + NORM_EPSILON)).astype(jnp.bfloat16)
    for iteration in range(NS_STEPS):
        gram_mat = jnp.einsum(
            "skab,skac->skbc", polar_map, polar_map, preferred_element_type=jnp.float32
        ).astype(jnp.bfloat16)
        product = jnp.einsum(
            "skab,skbc->skac", polar_map, gram_mat, preferred_element_type=jnp.float32
        )
        polar_map = (1.5 * polar_map.astype(jnp.float32) - 0.5 * product).astype(jnp.bfloat16)
    mapped = jnp.einsum(
        "sfka,skab->sfkb", subj_tiles, polar_map, preferred_element_type=jnp.float32
    )
    tiles = mapped.reshape(subj_count, frame_count, BLK_DEV * 3, BLOCK)
    one_hot = (window_ids[:, None] == jnp.arange(window_blocks, dtype=jnp.int32)[None, :]).astype(
        jnp.float32
    )
    window_sum = jnp.einsum("sfjc,jw->sfwc", tiles, one_hot, precision=lax.Precision.HIGHEST)
    window_sum = window_sum.reshape(subj_count, frame_count, 3, width_dev)
    mine = position * BLK_DEV + jnp.arange(BLK_DEV, dtype=jnp.int32)
    block_ids = all_lists.reshape(-1)
    coverage = jnp.sum((block_ids[:, None] == mine[None, :]).astype(jnp.float32), axis=0)
    per_vertex = jnp.repeat(coverage, BLOCK)
    subject_sum = jnp.sum(window_sum, axis=0)
    from_lower = from_behind(subject_sum[:, 2].astype(jnp.bfloat16), "cortex", 1).astype(
        jnp.float32
    )
    from_upper = from_behind(subject_sum[:, 0].astype(jnp.bfloat16), "cortex", -1).astype(
        jnp.float32
    )
    own_sum = subject_sum[:, 1] + from_lower + from_upper
    averaged = own_sum / per_vertex[None, :]
    combined = lax.psum(averaged, "subj")
    return combined / (subj_count * lax.axis_size("subj"))


def solution(mesh):
    in_specs = (P("subj", None, "cortex"), P(None, "cortex"), P("cortex", None))
    out_specs = P(None, "cortex")
    return jax.shard_map(body, mesh=mesh, in_specs=in_specs, out_specs=out_specs, check_vma=False)
```

profile of v0, /device:TPU:32, one launch (start us, length us, event | category | flops | bytes accessed | tf_op | source)
XLA Modules:
  0.0 224.9 jit_solution(2787901281315363890)
XLA Ops:
  6.5 1.3 copy.147
  7.9 1.9 collective-permute-start.1
  9.8 2.4 %collective-permute-start = (bf16[1024,256]{0,1:T(8,128)(2,1)S(1)}, bf16[1024,256]{0,1:T(8,128)(2,1)}, u32[]{:S(2)}, u32[]{:S(2)}) collective-permute-start(bf16[1024,256]{0,1:T(8,128)(2,1)S(1)} %copy.147), channel_id=1, source_target_pairs={{0,1},{1,2},{2,3},{3,4},{4,5},{5,6},{6,7},{7,8},{8,9},{9,10},{10,1... | collective-permute-start | bytes 1572872 | tf_op jit(solution)/shard_map/ppermute | solution.py:21
  13.5 3.4 %collective-permute-start.3 = (bf16[2,1024,256]{1,2,0:T(8,128)(2,1)}, bf16[2,1024,256]{1,2,0:T(8,128)(2,1)}, u32[]{:S(2)}, u32[]{:S(2)}) collective-permute-start(bf16[2,1024,256]{1,2,0:T(8,128)(2,1)} %copy.152), channel_id=1, source_target_pairs={{1,0},{2,1},{3,2},{4,3},{5,4},{6,5},{7,6},{8,7},{9,8},{10,9},{11,1... | collective-permute-start | bytes 3145736 | tf_op jit(solution)/shard_map/ppermute | solution.py:23
  16.9 2.0 collective-permute-start.2
  20.9 1.3 pad_maximum_fusion.1
  24.7 1.4 bitcast_select_fusion.1
  26.0 3.5 %collective-permute-done.3 = bf16[2,1024,256]{1,2,0:T(8,128)(2,1)} collective-permute-done((bf16[2,1024,256]{1,2,0:T(8,128)(2,1)}, bf16[2,1024,256]{1,2,0:T(8,128)(2,1)}, u32[]{:S(2)}, u32[]{:S(2)}) %collective-permute-start.3) | collective-permute-done | bytes 1048608 | tf_op jit(solution)/shard_map/ppermute | solution.py:23
  29.5 3.8 %collective-permute-done.2 = bf16[2,1024,256]{1,2,0:T(8,128)(2,1)} collective-permute-done((bf16[2,1024,256]{1,2,0:T(8,128)(2,1)}, bf16[2,1024,256]{1,2,0:T(8,128)(2,1)}, u32[]{:S(2)}, u32[]{:S(2)}) %collective-permute-start.2) | collective-permute-done | bytes 1048608 | tf_op jit(solution)/shard_map/ppermute | solution.py:21
  33.4 3.1 %pad_maximum_fusion = bf16[2,1024,768]{1,2,0:T(8,128)(2,1)} fusion(bf16[2,1024,256]{1,2,0:T(8,128)(2,1)} %collective-permute-done.3, bf16[2,1024,256]{1,2,0:T(8,128)(2,1)} %copy.152, bf16[2,1024,256]{1,2,0:T(8,128)(2,1)} %collective-permute-done.2), kind=kLoop, calls=%fused_computation.2 | loop fusion | flops 9437184 | bytes 6291456 | tf_op jit(solution)/shard_map/concatenate | solution.py:19
  36.5 3.5 %copy.155 = bf16[2,1024,6,128]{3,1,2,0:T(8,128)(2,1)S(1)} copy(bf16[2,1024,6,128]{1,3,2,0:T(8,128)(2,1)} %bitcast.71) | data formatting | bytes 6291456 | tf_op jit(solution)/shard_map/reshape | solution.py:61
  40.0 2.7 %gather_fusion.1 = bf16[6,2,1024,128]{3,2,1,0:T(8,128)(2,1)} fusion(bf16[2,1024,6,128]{3,1,2,0:T(8,128)(2,1)S(1)} %copy.155, s32[1024]{0:T(1024)S(1)} %pad_clamp_fusion), kind=kCustom, calls=%fused_computation.1 | custom fusion | bytes 6291480 | tf_op jit(solution)/shard_map/jit(_take)/gather | solution.py:63
  42.7 3.4 %copy.156 = bf16[2,1024,6,128]{1,3,2,0:T(8,128)(2,1)S(1)} copy(bf16[2,1024,6,128]{3,1,0,2:T(8,128)(2,1)} %bitcast.69) | data formatting | bytes 6291456 | tf_op jit(solution)/shard_map/jit(_take)/gather | solution.py:63
  47.6 1.7 multiply_reduce_fusion
  65.5 4.5 %fusion.10 = f32[2,2,384,1024]{3,2,1,0:T(8,128)} fusion(bf16[2,1024,2,384]{1,3,2,0:T(8,128)(2,1)S(1)} %bitcast_select_fusion, bf16[2,2,384,384]{2,3,0,1:T(8,128)(2,1)S(1)} %subtract_convert_fusion), kind=kOutput, calls=%fused_computation.36 | convolution fusion | flops 1207959552 | bytes 10616832 | tf_op jit(solution)/shard_map/sfka,skab->sfkb/dot_general | solution.py:82
  70.0 8.2 %copy.193 = f32[2,1024,6,128]{3,2,1,0:T(8,128)} copy(f32[2,1024,6,128]{1,3,2,0:T(8,128)} %bitcast.66) | data formatting | bytes 12582912 | tf_op jit(solution)/shard_map/reshape | solution.py:85
  78.2 10.5 %convolution_reduce_fusion = f32[6,1024,128]{2,0,1:T(8,128)} fusion(f32[2,1024,6,128]{3,2,1,0:T(8,128)} %copy.193, s32[6]{0:T(128)S(1)} %eq.37), kind=kOutput, calls=%fused_computation.6 | convolution fusion | flops 114032672 | bytes 9437208 | tf_op jit(solution)/shard_map/sfjc,jw->sfwc/dot_general | solution.py:89
  88.6 3.7 %copy.194 = f32[1024,6,128]{0,2,1:T(8,128)S(1)} copy(f32[1024,6,128]{2,1,0:T(8,128)} %bitcast.70) | data formatting | bytes 6291456 | tf_op jit(solution)/shard_map/reduce_sum | solution.py:95
  93.6 1.9 collective-permute-start.4
  95.5 3.6 %collective-permute-start.5 = (bf16[1024,256]{0,1:T(8,128)(2,1)}, bf16[1024,256]{0,1:T(8,128)(2,1)}, u32[]{:S(2)}, u32[]{:S(2)}) collective-permute-start(bf16[1024,256]{0,1:T(8,128)(2,1)} %get-tuple-element.8), channel_id=1, source_target_pairs={{1,0},{2,1},{3,2},{4,3},{5,4},{6,5},{7,6},{8,7},{9,8},{10,9},{11,1... | collective-permute-start | bytes 1572872 | tf_op jit(solution)/shard_map/ppermute | solution.py:48
  99.8 14.4 %all-to-all-start = ((s32[32,2,3]{2,1,0:T(2,128)}), s32[32,2,3]{2,1,0:T(2,128)S(1)}, u32[]{:S(2)}, u32[]{:S(2)}) async-start(s32[32,2,3]{2,1,0:T(2,128)} %broadcast_in_dim.43), calls=%async_computation | async-start | bytes 65536 | tf_op jit(solution)/shard_map/all_to_all | solution.py:38
  114.2 7.3 %all-to-all-done = s32[32,2,3]{2,1,0:T(2,128)S(1)} async-done(((s32[32,2,3]{2,1,0:T(2,128)}), s32[32,2,3]{2,1,0:T(2,128)S(1)}, u32[]{:S(2)}, u32[]{:S(2)}) %all-to-all-start) | async-done | bytes 800 | tf_op jit(solution)/shard_map/all_to_all | solution.py:38
  122.0 2.4 %fusion.23 = f32[1024,256]{0,1:T(8,128)} fusion(f32[1024,3,256]{0,2,1:T(8,128)S(1)} %bitcast.68, bf16[1024,256]{0,1:T(8,128)(2,1)} %collective-permute-done.5, bf16[1024,256]{0,1:T(8,128)(2,1)} %collective-permute-done.4, f32[256]{0:T(256)S(1)} %broadcast_bitcast_fusion.1), kind=kLoop, calls=%fused_computation.50 | loop fusion | flops 1310720 | bytes 3146752 | tf_op jit(solution)/shard_map/div | solution.py:103
  124.4 91.1 %all-reduce.2.cloned.1.call-done = f32[1024,256]{0,1:T(8,128)} async-done(((f32[1024,256]{0,1:T(8,128)}), f32[1024,256]{0,1:T(8,128)}) %all-reduce.2.cloned.1.call-update) | async-done | bytes 1048592 | tf_op jit(solution)/shard_map/psum | solution.py:104
  (56 shorter events, 28.3 us)
Async XLA Ops:
  6.5 5.7 %copy-start.2 = (bf16[2,1024,256]{2,1,0:T(8,128)(2,1)S(1)}, bf16[2,1024,256]{2,1,0:T(8,128)(2,1)}, u32[]{:S(2)}) copy-start(bf16[2,1024,256]{2,1,0:T(8,128)(2,1)} %param.3) | copy-start | bytes 3145732
  6.5 12.4 %copy-start.4 = (s32[2,3]{1,0:T(2,128)S(1)}, s32[2,3]{1,0:T(2,128)}, u32[]{:S(2)}) copy-start(s32[2,3]{1,0:T(2,128)} %param.5) | copy-start | bytes 76
  7.9 12.2 %collective-permute-start.1 = (bf16[1024,256]{0,1:T(8,128)(2,1)S(1)}, bf16[1024,256]{0,1:T(8,128)(2,1)S(1)}, u32[]{:S(2)}, u32[]{:S(2)}) collective-permute-start(bf16[1024,256]{0,1:T(8,128)(2,1)S(1)} %copy.147), channel_id=1, source_target_pairs={{1,0},{2,1},{3,2},{4,3},{5,4},{6,5},{7,6},{8,7},{9,8},{10,9},{11,1... | collective-permute-start | bytes 1572872 | tf_op jit(solution)/shard_map/ppermute | solution.py:23
  9.8 11.1 %collective-permute-start = (bf16[1024,256]{0,1:T(8,128)(2,1)S(1)}, bf16[1024,256]{0,1:T(8,128)(2,1)}, u32[]{:S(2)}, u32[]{:S(2)}) collective-permute-start(bf16[1024,256]{0,1:T(8,128)(2,1)S(1)} %copy.147), channel_id=1, source_target_pairs={{0,1},{1,2},{2,3},{3,4},{4,5},{5,6},{6,7},{7,8},{8,9},{9,10},{10,1... | collective-permute-start | bytes 1572872 | tf_op jit(solution)/shard_map/ppermute | solution.py:21
  13.5 16.0 %collective-permute-start.3 = (bf16[2,1024,256]{1,2,0:T(8,128)(2,1)}, bf16[2,1024,256]{1,2,0:T(8,128)(2,1)}, u32[]{:S(2)}, u32[]{:S(2)}) collective-permute-start(bf16[2,1024,256]{1,2,0:T(8,128)(2,1)} %copy.152), channel_id=1, source_target_pairs={{1,0},{2,1},{3,2},{4,3},{5,4},{6,5},{7,6},{8,7},{9,8},{10,9},{11,1... | collective-permute-start | bytes 3145736 | tf_op jit(solution)/shard_map/ppermute | solution.py:23
  16.9 16.4 %collective-permute-start.2 = (bf16[2,1024,256]{1,2,0:T(8,128)(2,1)}, bf16[2,1024,256]{1,2,0:T(8,128)(2,1)}, u32[]{:S(2)}, u32[]{:S(2)}) collective-permute-start(bf16[2,1024,256]{1,2,0:T(8,128)(2,1)} %copy.152), channel_id=1, source_target_pairs={{0,1},{1,2},{2,3},{3,4},{4,5},{5,6},{6,7},{7,8},{8,9},{9,10},{10,1... | collective-permute-start | bytes 3145736 | tf_op jit(solution)/shard_map/ppermute | solution.py:21
  20.1 0.8 copy-start.3
  46.0 1.1 copy-start
  46.1 1.6 copy-start.1
  93.6 28.4 %collective-permute-start.4 = (bf16[1024,256]{0,1:T(8,128)(2,1)}, bf16[1024,256]{0,1:T(8,128)(2,1)}, u32[]{:S(2)}, u32[]{:S(2)}) collective-permute-start(bf16[1024,256]{0,1:T(8,128)(2,1)} %get-tuple-element.7), channel_id=1, source_target_pairs={{0,1},{1,2},{2,3},{3,4},{4,5},{5,6},{6,7},{7,8},{8,9},{9,10},{10,1... | collective-permute-start | bytes 1572872 | tf_op jit(solution)/shard_map/ppermute | solution.py:48
  95.5 26.5 %collective-permute-start.5 = (bf16[1024,256]{0,1:T(8,128)(2,1)}, bf16[1024,256]{0,1:T(8,128)(2,1)}, u32[]{:S(2)}, u32[]{:S(2)}) collective-permute-start(bf16[1024,256]{0,1:T(8,128)(2,1)} %get-tuple-element.8), channel_id=1, source_target_pairs={{1,0},{2,1},{3,2},{4,3},{5,4},{6,5},{7,6},{8,7},{9,8},{10,9},{11,1... | collective-permute-start | bytes 1572872 | tf_op jit(solution)/shard_map/ppermute | solution.py:48
  99.8 21.8 %all-to-all-start = ((s32[32,2,3]{2,1,0:T(2,128)}), s32[32,2,3]{2,1,0:T(2,128)S(1)}, u32[]{:S(2)}, u32[]{:S(2)}) async-start(s32[32,2,3]{2,1,0:T(2,128)} %broadcast_in_dim.43), calls=%async_computation | async-start | bytes 65536 | tf_op jit(solution)/shard_map/all_to_all | solution.py:38
  114.2 101.3 %all-reduce.2.cloned.1.call-start = ((), (), s32[]{:S(2)}) async-start(), calls=%async_computation.1 | async-start | bytes 2097152 | tf_op jit(solution)/shard_map/psum | solution.py:104
Sparse Core Ops, SparseCore 0:
  124.5 90.8 all-reduce.1
where the time goes:
time: 226 us; the launch traced here: 225 us
  waiting for transfers between devices  106 us (47%)
  matrix products  32.1 us (14%)
  local copies, waits for them, and re-layouts  32 us (14%)
  starting transfers between devices  29.7 us (13%)
  between operations  13.7 us (6%)
  other arithmetic  11.7 us (5%)
    psum x1, waiting for transfers between devices, body(): combined = lax.psum(averaged, 'subj')  91.1 us
    all_to_all x1, starting transfers between devices, copy_for_each(): lax.all_to_all(jnp.broadcast_to(x[None], (length, *x.shape)), axis, 0, 0,...  14.4 us
    dot_general x1, matrix products, body(): jnp.einsum('sfjc,jw->sfwc', tiles, one_hot, precision=lax.Precision.HIGHEST)  10.5 us
    reshape x1, local copies, waits for them, and re-layouts, body(): tiles = mapped.reshape(subj_count, frame_count, BLK_DEV * 3, BLOCK)  8.2 us
    dot_general x8, matrix products, body(): jnp.einsum('skab,skbc->skac', polar_map, gram_mat, preferred_element_type...  8.04 us
    dot_general x8, matrix products, body(): jnp.einsum('skab,skac->skbc', polar_map, polar_map, preferred_element_typ...  7.46 us
    all_to_all x1, waiting for transfers between devices, copy_for_each(): lax.all_to_all(jnp.broadcast_to(x[None], (length, *x.shape)), axis, 0, 0,...  7.34 us
    gather x2, local copies, waits for them, and re-layouts, body(): jnp.take(data_blocks, window_ids, axis=2)  6.08 us
  transfers between devices with their start and end apart: 8, of which 4 were waited for; matrix products, arithmetic and copies ran while one was open for 4% of the time, Pallas kernels for 0%

commit v1 on v0

--- a/solution.py
+++ b/solution.py
@@ -101,7 +101,7 @@
     )
     own_sum = subject_sum[:, 1] + from_lower + from_upper
     averaged = own_sum / per_vertex[None, :]
-    combined = lax.psum(averaged, "subj")
+    combined = jnp.sum(lax.all_gather(averaged, "subj"), axis=0)
     return combined / (subj_count * lax.axis_size("subj"))
 
 

time: 226 us -> 263 us (1.16); the launches traced: 225 us -> 259 us
  waiting for transfers between devices: 106 us -> 127 us
  local copies, waits for them, and re-layouts: 32 us -> 43.4 us
    all_gather x0 -> x1, waiting for transfers between devices: none -> 112 us  [body(): combined = jnp.sum(lax.all_gather(averaged, 'subj'), axis=0)]
    psum x1 -> x0, waiting for transfers between devices: 91.1 us -> none  [body(): combined = lax.psum(averaged, 'subj')]
    unnamed x14 -> x15, local copies, waits for them, and re-layouts: 4.76 us -> 15.7 us
  transfers between devices with their start and end apart: 8 -> 8, of which waited for: 4 -> 4; matrix products, arithmetic and copies ran while one was open for 4% -> 3% of each run, Pallas kernels for 0% -> 0%
where the time goes in v1:
time: 263 us; the launch traced here: 259 us
  waiting for transfers between devices  127 us (48%)
  local copies, waits for them, and re-layouts  43.4 us (17%)
  matrix products  32.1 us (12%)
  starting transfers between devices  29.7 us (11%)
  between operations  14 us (5%)
  other arithmetic  12.5 us (5%)
    all_gather x1, waiting for transfers between devices, body(): combined = jnp.sum(lax.all_gather(averaged, 'subj'), axis=0)  112 us
    unnamed x15, local copies, waits for them, and re-layouts  15.7 us
    all_to_all x1, starting transfers between devices, copy_for_each(): lax.all_to_all(jnp.broadcast_to(x[None], (length, *x.shape)), axis, 0, 0,...  14.4 us
    dot_general x1, matrix products, body(): jnp.einsum('sfjc,jw->sfwc', tiles, one_hot, precision=lax.Precision.HIGHEST)  10.5 us
    reshape x1, local copies, waits for them, and re-layouts, body(): tiles = mapped.reshape(subj_count, frame_count, BLK_DEV * 3, BLOCK)  8.2 us
    dot_general x8, matrix products, body(): jnp.einsum('skab,skbc->skac', polar_map, gram_mat, preferred_element_type...  8 us
    dot_general x8, matrix products, body(): jnp.einsum('skab,skac->skbc', polar_map, polar_map, preferred_element_typ...  7.44 us
    all_to_all x1, waiting for transfers between devices, copy_for_each(): lax.all_to_all(jnp.broadcast_to(x[None], (length, *x.shape)), axis, 0, 0,...  7.34 us
  transfers between devices with their start and end apart: 8, of which 4 were waited for; matrix products, arithmetic and copies ran while one was open for 3% of the time, Pallas kernels for 0%

profile of v1, /device:TPU:32, one launch (start us, length us, event | category | flops | bytes accessed | tf_op | source)
XLA Modules:
  0.0 258.7 jit_solution(8567660432652322029)
XLA Ops:
  7.9 1.9 collective-permute-start.1
  9.8 2.4 collective-permute-start
  13.5 3.4 %collective-permute-start.3 = (bf16[2,1024,256]{1,2,0:T(8,128)(2,1)}, bf16[2,1024,256]{1,2,0:T(8,128)(2,1)}, u32[]{:S(2)}, u32[]{:S(2)}) collective-permute-start(bf16[2,1024,256]{1,2,0:T(8,128)(2,1)} %copy.158), channel_id=1, source_target_pairs={{1,0},{2,1},{3,2},{4,3},{5,4},{6,5},{7,6},{8,7},{9,8},{10,9},{11,1... | collective-permute-start | bytes 3145736 | tf_op jit(solution)/shard_map/ppermute | solution.py:23
  16.9 2.0 collective-permute-start.2
  24.7 1.4 bitcast_select_fusion.1
  26.0 3.5 %collective-permute-done.3 = bf16[2,1024,256]{1,2,0:T(8,128)(2,1)} collective-permute-done((bf16[2,1024,256]{1,2,0:T(8,128)(2,1)}, bf16[2,1024,256]{1,2,0:T(8,128)(2,1)}, u32[]{:S(2)}, u32[]{:S(2)}) %collective-permute-start.3) | collective-permute-done | bytes 1048608 | tf_op jit(solution)/shard_map/ppermute | solution.py:23
  29.5 3.8 %collective-permute-done.2 = bf16[2,1024,256]{1,2,0:T(8,128)(2,1)} collective-permute-done((bf16[2,1024,256]{1,2,0:T(8,128)(2,1)}, bf16[2,1024,256]{1,2,0:T(8,128)(2,1)}, u32[]{:S(2)}, u32[]{:S(2)}) %collective-permute-start.2) | collective-permute-done | bytes 1048608 | tf_op jit(solution)/shard_map/ppermute | solution.py:21
  33.4 3.1 %pad_maximum_fusion = bf16[2,1024,768]{1,2,0:T(8,128)(2,1)} fusion(bf16[2,1024,256]{1,2,0:T(8,128)(2,1)} %collective-permute-done.3, bf16[2,1024,256]{1,2,0:T(8,128)(2,1)} %copy.158, bf16[2,1024,256]{1,2,0:T(8,128)(2,1)} %collective-permute-done.2), kind=kLoop, calls=%fused_computation.3 | loop fusion | flops 9437184 | bytes 6291456 | tf_op jit(solution)/shard_map/concatenate | solution.py:19
  36.5 3.5 %copy.161 = bf16[2,1024,6,128]{3,1,2,0:T(8,128)(2,1)S(1)} copy(bf16[2,1024,6,128]{1,3,2,0:T(8,128)(2,1)} %bitcast.76) | data formatting | bytes 6291456 | tf_op jit(solution)/shard_map/reshape | solution.py:61
  40.0 2.7 %gather_fusion.1 = bf16[6,2,1024,128]{3,2,1,0:T(8,128)(2,1)} fusion(bf16[2,1024,6,128]{3,1,2,0:T(8,128)(2,1)S(1)} %copy.161, s32[1024]{0:T(1024)S(1)} %pad_clamp_fusion), kind=kCustom, calls=%fused_computation.1 | custom fusion | bytes 6291480 | tf_op jit(solution)/shard_map/jit(_take)/gather | solution.py:63
  42.7 3.7 %copy.162 = bf16[2,1024,6,128]{1,3,2,0:T(8,128)(2,1)S(1)} copy(bf16[2,1024,6,128]{3,1,0,2:T(8,128)(2,1)} %bitcast.74) | data formatting | bytes 6291456 | tf_op jit(solution)/shard_map/jit(_take)/gather | solution.py:63
  47.9 1.7 multiply_reduce_fusion
  65.7 4.5 %fusion.10 = f32[2,2,384,1024]{3,2,1,0:T(8,128)} fusion(bf16[2,1024,2,384]{1,3,2,0:T(8,128)(2,1)S(1)} %bitcast_select_fusion, bf16[2,2,384,384]{2,3,0,1:T(8,128)(2,1)S(1)} %subtract_convert_fusion), kind=kOutput, calls=%fused_computation.37 | convolution fusion | flops 1207959552 | bytes 10616832 | tf_op jit(solution)/shard_map/sfka,skab->sfkb/dot_general | solution.py:82
  70.2 8.2 %copy.199 = f32[2,1024,6,128]{3,2,1,0:T(8,128)} copy(f32[2,1024,6,128]{1,3,2,0:T(8,128)} %bitcast.71) | data formatting | bytes 12582912 | tf_op jit(solution)/shard_map/reshape | solution.py:85
  78.4 10.5 %convolution_reduce_fusion = f32[6,1024,128]{2,0,1:T(8,128)} fusion(f32[2,1024,6,128]{3,2,1,0:T(8,128)} %copy.199, s32[6]{0:T(128)S(1)} %eq.37), kind=kOutput, calls=%fused_computation.7 | convolution fusion | flops 114032672 | bytes 9437208 | tf_op jit(solution)/shard_map/sfjc,jw->sfwc/dot_general | solution.py:89
  88.9 3.9 %copy.200 = f32[1024,6,128]{0,2,1:T(8,128)S(1)} copy(f32[1024,6,128]{2,1,0:T(8,128)} %bitcast.75) | data formatting | bytes 6291456 | tf_op jit(solution)/shard_map/reduce_sum | solution.py:95
  94.0 1.9 collective-permute-start.4
  95.9 3.6 %collective-permute-start.5 = (bf16[1024,256]{0,1:T(8,128)(2,1)}, bf16[1024,256]{0,1:T(8,128)(2,1)}, u32[]{:S(2)}, u32[]{:S(2)}) collective-permute-start(bf16[1024,256]{0,1:T(8,128)(2,1)} %get-tuple-element.8), channel_id=1, source_target_pairs={{1,0},{2,1},{3,2},{4,3},{5,4},{6,5},{7,6},{8,7},{9,8},{10,9},{11,1... | collective-permute-start | bytes 1572872 | tf_op jit(solution)/shard_map/ppermute | solution.py:48
  100.2 14.4 %all-to-all-start = ((s32[32,2,3]{2,1,0:T(2,128)}), s32[32,2,3]{2,1,0:T(2,128)S(1)}, u32[]{:S(2)}, u32[]{:S(2)}) async-start(s32[32,2,3]{2,1,0:T(2,128)} %broadcast_in_dim.43), calls=%async_computation | async-start | bytes 65536 | tf_op jit(solution)/shard_map/all_to_all | solution.py:38
  114.7 7.3 %all-to-all-done = s32[32,2,3]{2,1,0:T(2,128)S(1)} async-done(((s32[32,2,3]{2,1,0:T(2,128)}), s32[32,2,3]{2,1,0:T(2,128)S(1)}, u32[]{:S(2)}, u32[]{:S(2)}) %all-to-all-start) | async-done | bytes 800 | tf_op jit(solution)/shard_map/all_to_all | solution.py:38
  122.4 2.4 fusion.23
  124.9 112.4 %all-gather.3.cloned.1.call-done = f32[8192,256]{0,1:T(8,128)} async-done(((f32[1024,256]{0,1:T(8,128)}), f32[8192,256]{0,1:T(8,128)}) %all-gather.3.cloned.1.call-update) | async-done | bytes 8388624 | tf_op jit(solution)/shard_map/all_gather | solution.py:104
  237.3 10.9 %copy.250 = f32[32,8,8,1024]{3,2,1,0:T(8,128)S(1)} copy(f32[32,8,8,1024]{3,1,2,0:T(8,128)} %bitcast.79) | data formatting | bytes 16777216
  248.2 2.0 bitcast_reduce_fusion
  (58 shorter events, 29.7 us)
Async XLA Ops:
  6.5 5.7 %copy-start.2 = (bf16[2,1024,256]{2,1,0:T(8,128)(2,1)S(1)}, bf16[2,1024,256]{2,1,0:T(8,128)(2,1)}, u32[]{:S(2)}) copy-start(bf16[2,1024,256]{2,1,0:T(8,128)(2,1)} %param.3) | copy-start | bytes 3145732
  6.5 12.4 %copy-start.4 = (s32[2,3]{1,0:T(2,128)S(1)}, s32[2,3]{1,0:T(2,128)}, u32[]{:S(2)}) copy-start(s32[2,3]{1,0:T(2,128)} %param.5) | copy-start | bytes 76
  7.9 12.2 %collective-permute-start.1 = (bf16[1024,256]{0,1:T(8,128)(2,1)S(1)}, bf16[1024,256]{0,1:T(8,128)(2,1)S(1)}, u32[]{:S(2)}, u32[]{:S(2)}) collective-permute-start(bf16[1024,256]{0,1:T(8,128)(2,1)S(1)} %copy.153), channel_id=1, source_target_pairs={{1,0},{2,1},{3,2},{4,3},{5,4},{6,5},{7,6},{8,7},{9,8},{10,9},{11,1... | collective-permute-start | bytes 1572872 | tf_op jit(solution)/shard_map/ppermute | solution.py:23
  9.8 11.1 %collective-permute-start = (bf16[1024,256]{0,1:T(8,128)(2,1)S(1)}, bf16[1024,256]{0,1:T(8,128)(2,1)}, u32[]{:S(2)}, u32[]{:S(2)}) collective-permute-start(bf16[1024,256]{0,1:T(8,128)(2,1)S(1)} %copy.153), channel_id=1, source_target_pairs={{0,1},{1,2},{2,3},{3,4},{4,5},{5,6},{6,7},{7,8},{8,9},{9,10},{10,1... | collective-permute-start | bytes 1572872 | tf_op jit(solution)/shard_map/ppermute | solution.py:21
  13.5 16.0 %collective-permute-start.3 = (bf16[2,1024,256]{1,2,0:T(8,128)(2,1)}, bf16[2,1024,256]{1,2,0:T(8,128)(2,1)}, u32[]{:S(2)}, u32[]{:S(2)}) collective-permute-start(bf16[2,1024,256]{1,2,0:T(8,128)(2,1)} %copy.158), channel_id=1, source_target_pairs={{1,0},{2,1},{3,2},{4,3},{5,4},{6,5},{7,6},{8,7},{9,8},{10,9},{11,1... | collective-permute-start | bytes 3145736 | tf_op jit(solution)/shard_map/ppermute | solution.py:23
  16.9 16.4 %collective-permute-start.2 = (bf16[2,1024,256]{1,2,0:T(8,128)(2,1)}, bf16[2,1024,256]{1,2,0:T(8,128)(2,1)}, u32[]{:S(2)}, u32[]{:S(2)}) collective-permute-start(bf16[2,1024,256]{1,2,0:T(8,128)(2,1)} %copy.158), channel_id=1, source_target_pairs={{0,1},{1,2},{2,3},{3,4},{4,5},{5,6},{6,7},{7,8},{8,9},{9,10},{10,1... | collective-permute-start | bytes 3145736 | tf_op jit(solution)/shard_map/ppermute | solution.py:21
  20.1 0.8 copy-start.3
  46.3 1.1 copy-start
  46.3 1.6 copy-start.1
  94.0 28.4 %collective-permute-start.4 = (bf16[1024,256]{0,1:T(8,128)(2,1)}, bf16[1024,256]{0,1:T(8,128)(2,1)}, u32[]{:S(2)}, u32[]{:S(2)}) collective-permute-start(bf16[1024,256]{0,1:T(8,128)(2,1)} %get-tuple-element.7), channel_id=1, source_target_pairs={{0,1},{1,2},{2,3},{3,4},{4,5},{5,6},{6,7},{7,8},{8,9},{9,10},{10,1... | collective-permute-start | bytes 1572872 | tf_op jit(solution)/shard_map/ppermute | solution.py:48
  95.9 26.5 %collective-permute-start.5 = (bf16[1024,256]{0,1:T(8,128)(2,1)}, bf16[1024,256]{0,1:T(8,128)(2,1)}, u32[]{:S(2)}, u32[]{:S(2)}) collective-permute-start(bf16[1024,256]{0,1:T(8,128)(2,1)} %get-tuple-element.8), channel_id=1, source_target_pairs={{1,0},{2,1},{3,2},{4,3},{5,4},{6,5},{7,6},{8,7},{9,8},{10,9},{11,1... | collective-permute-start | bytes 1572872 | tf_op jit(solution)/shard_map/ppermute | solution.py:48
  100.2 21.8 %all-to-all-start = ((s32[32,2,3]{2,1,0:T(2,128)}), s32[32,2,3]{2,1,0:T(2,128)S(1)}, u32[]{:S(2)}, u32[]{:S(2)}) async-start(s32[32,2,3]{2,1,0:T(2,128)} %broadcast_in_dim.43), calls=%async_computation | async-start | bytes 65536 | tf_op jit(solution)/shard_map/all_to_all | solution.py:38
  114.6 122.6 %all-gather.3.cloned.1.call-start = ((), (), s32[]{:S(2)}) async-start(), calls=%async_computation.1 | async-start | bytes 9437184 | tf_op jit(solution)/shard_map/all_gather | solution.py:104
Sparse Core Ops, SparseCore 0:
  125.0 112.2 all-gather.2
